TPU v7x, 32 devices: a whole 2x2x4 slice. The times are simulated.
32 devices in a mesh: row: 4 (over y, x), col: 8 (over z, core).
Axes of the slice: x: 2, y: 2, z: 4, core: 2. Of those that a mesh axis runs over, the one named last changes fastest.
Arguments:
- right_side: float32 [512, 128], P('row'), may hold values from -6 to 6
- factor_window: float32 [512, 512], P('row', 'col'), may hold values from -0.1875 to 0.1875
- diag_inverse: float32 [512, 128], P('row'), as said below
- phase_cov: bfloat16 [512, 16384], P('col', 'row'), may hold values from -0.25 to 0.25
Outputs:
- basis: float32 [32, 512, 128], P('row', 'col')
- solved: float32 [512, 128], P('col')
Inputs may be any that keep to these rules, and one draw needn't show every extreme that they name: `diag_inverse`: each block of 128 rows is a lower triangular matrix with a diagonal between 0.5 and 2.
All inputs are finite; a program needn't handle non-finite values.
Results may differ from a plain program's by a relative error of at most 0.0043.
Values sent between devices are 32-bit elements; how exact they have to be, the bound alone decides.
A program may use at most 64 MiB of HBM per device.

v0:
```python
import jax
import jax.numpy as jnp
from jax import lax
from jax.sharding import PartitionSpec as P

TILE_ROWS = 512


def from_root(block, axis, owner):
    block = jnp.where(lax.axis_index(axis) == owner, block, jnp.zeros_like(block))
    return lax.psum(block, axis)


def tile_basis(lower, tile):
    return jax.scipy.linalg.solve_triangular(lower, tile.T, lower=True).T


def finish_tiles(gram, tiles):
    lower = jnp.linalg.cholesky(gram)
    return jax.vmap(tile_basis)(lower, tiles)


def local(right_side, factor_window, diag_inverse, phase_cov):
    row_count = lax.axis_size("row")
    col_count = lax.axis_size("col")
    col_index = lax.axis_index("col")
    block_rows = right_side.shape[0]
    rank_width = right_side.shape[1]
    col_width = factor_window.shape[1]
    col_ratio = col_count // row_count
    row_offset = col_index % col_ratio * col_width
    owner_block = col_index // col_ratio
    partial_value = jnp.zeros((block_rows, rank_width), jnp.float32)
    own_solved = jnp.zeros((col_width, rank_width), jnp.float32)
    for block_index in range(row_count):
        summed = lax.psum(partial_value, "col")
        remaining = right_side - summed
        solved_full = jnp.dot(
            diag_inverse,
            remaining,
            precision=lax.Precision.HIGHEST,
            preferred_element_type=jnp.float32,
        )
        received = from_root(solved_full, "row", block_index)
        column_piece = lax.dynamic_slice_in_dim(received, row_offset, col_width, 0)
        owns_block = owner_block == block_index
        own_solved = jnp.where(owns_block, column_piece, own_solved)
        partial_value = lax.cond(
            owns_block,
            lambda running: running
            + jnp.dot(
                factor_window,
                column_piece,
                precision=lax.Precision.HIGHEST,
                preferred_element_type=jnp.float32,
            ),
            lambda running: running,
            partial_value,
        )
    solved_low = own_solved.astype(jnp.bfloat16)
    tile_count = phase_cov.shape[1] // TILE_ROWS
    cov_tiles = phase_cov.reshape(col_width, tile_count, TILE_ROWS)
    whole_tiles = lax.psum_scatter(
        jnp.einsum("kts,kr->tsr", cov_tiles, solved_low, preferred_element_type=jnp.float32),
        "col",
        scatter_dimension=0,
        tiled=True,
    )
    gram = jnp.einsum("tsr,tsq->trq", whole_tiles, whole_tiles, precision=lax.Precision.HIGHEST)
    tile_bases = finish_tiles(gram, whole_tiles)
    basis = lax.all_to_all(tile_bases, "col", split_axis=1, concat_axis=0, tiled=True)
    return (basis, own_solved)


def solution(mesh):
    in_specs = (P("row", None), P("row", "col"), P("row", None), P("col", "row"))
    out_specs = (P("row", "col", None), P("col", None))
    return jax.shard_map(local, mesh=mesh, in_specs=in_specs, out_specs=out_specs, check_vma=False)
```

profile of v0, /device:TPU:0, one launch (start us, length us, event | category | flops | bytes accessed | tf_op | source)
XLA Modules:
  0.0 444.9 jit_solution(12275134099939349102)
XLA Ops:
  7.2 0.0 copy-start
  7.2 0.0 copy-start.2
  7.2 0.0 all-reduce.8.cloned.1.call-start
  7.2 0.8 copy-done
  8.0 1.7 convolution_select_fusion.3
  9.7 0.0 all-reduce.8.cloned.1.call-update
  9.7 0.0 all-reduce.10.cloned.1.call-start
  9.8 46.2 %all-reduce.8.cloned.1.call-done = f32[128,128]{1,0:T(8,128)} async-done(((f32[128,128]{1,0:T(8,128)}), f32[128,128]{1,0:T(8,128)}) %all-reduce.8.cloned.1.call-update) | async-done | bytes 65552 | tf_op jit(solution)/shard_map/psum | solution.py:11
  56.0 0.8 constant_dynamic-slice_fusion.2
  56.8 1.0 conditional.3
  56.8 1.0 fusion.16
  57.8 0.0 copy-start.1
  57.8 0.6 copy-done.1
  58.5 0.0 all-reduce.10.cloned.1.call-update
  58.5 0.0 all-reduce.12.cloned.1.call-start
  58.5 55.1 %all-reduce.10.cloned.1.call-done = f32[128,128]{1,0:T(8,128)} async-done(((f32[128,128]{1,0:T(8,128)}), f32[128,128]{1,0:T(8,128)}) %all-reduce.10.cloned.1.call-update) | async-done | bytes 65552 | tf_op jit(solution)/shard_map/psum | solution.py:36
  113.6 1.7 fusion.2
  115.3 0.0 all-reduce.12.cloned.1.call-update
  115.4 0.0 all-reduce.14.cloned.1.call-start
  115.4 42.0 %all-reduce.12.cloned.1.call-done = f32[128,128]{1,0:T(8,128)} async-done(((f32[128,128]{1,0:T(8,128)}), f32[128,128]{1,0:T(8,128)}) %all-reduce.12.cloned.1.call-update) | async-done | bytes 65552 | tf_op jit(solution)/shard_map/psum | solution.py:11
  157.4 0.8 constant_dynamic-slice_fusion.1
  158.2 0.0 all-reduce.14.cloned.1.call-update
  158.2 0.0 all-reduce.16.cloned.1.call-start
  158.2 56.6 %all-reduce.14.cloned.1.call-done = f32[128,128]{1,0:T(8,128)} async-done(((f32[128,128]{1,0:T(8,128)}), f32[128,128]{1,0:T(8,128)}) %all-reduce.14.cloned.1.call-update) | async-done | bytes 65552 | tf_op jit(solution)/shard_map/psum | solution.py:36
  214.9 1.7 fusion.1
  216.6 0.0 all-reduce.16.cloned.1.call-update
  216.6 0.0 all-reduce.18.cloned.1.call-start
  216.7 41.8 %all-reduce.16.cloned.1.call-done = f32[128,128]{1,0:T(8,128)} async-done(((f32[128,128]{1,0:T(8,128)}), f32[128,128]{1,0:T(8,128)}) %all-reduce.16.cloned.1.call-update) | async-done | bytes 65552 | tf_op jit(solution)/shard_map/psum | solution.py:11
  258.5 0.8 constant_dynamic-slice_fusion
  259.3 0.0 all-reduce.18.cloned.1.call-update
  259.3 0.0 all-reduce.20.cloned.1.call-start
  259.3 56.6 %all-reduce.18.cloned.1.call-done = f32[128,128]{1,0:T(8,128)} async-done(((f32[128,128]{1,0:T(8,128)}), f32[128,128]{1,0:T(8,128)}) %all-reduce.18.cloned.1.call-update) | async-done | bytes 65552 | tf_op jit(solution)/shard_map/psum | solution.py:36
  316.0 1.7 fusion
  317.7 0.0 all-reduce.20.cloned.1.call-update
  317.7 0.0 reduce-scatter.2.cloned.1.call-start
  317.8 42.6 %all-reduce.20.cloned.1.call-done = f32[128,128]{1,0:T(8,128)} async-done(((f32[128,128]{1,0:T(8,128)}), f32[128,128]{1,0:T(8,128)}) %all-reduce.20.cloned.1.call-update) | async-done | bytes 65552 | tf_op jit(solution)/shard_map/psum | solution.py:11
  360.3 0.8 select_select_fusion.1
  361.1 0.0 copy-start.3
  361.1 0.0 copy-done.2
  361.2 1.8 convolution_bitcast_fusion
  362.9 0.0 reduce-scatter.2.cloned.1.call-update
  363.0 0.0 copy-done.3
  363.0 36.4 %reduce-scatter.2.cloned.1.call-done = f32[1,512,128]{1,2,0:T(8,128)} async-done(((f32[8,512,128]{1,2,0:T(8,128)}), f32[1,512,128]{1,2,0:T(8,128)}) %reduce-scatter.2.cloned.1.call-update) | async-done | bytes 262160 | tf_op jit(solution)/shard_map/reduce_scatter | solution.py:63
  399.3 1.4 fusion.6
  400.8 0.1 copy.37
  400.9 11.7 %custom-call.8 = f32[1,128,128]{2,1,0:T(8,128)S(1)} custom-call(f32[1,128,128]{2,1,0:T(8,128)S(1)} %fusion.9), custom_call_target="Cholesky" | custom-call | tf_op jit(solution)/shard_map/jit(cholesky)/cholesky | solution.py:19
  412.6 0.6 compare_reduce_fusion
  413.3 0.7 fusion.8
  413.9 9.8 %custom-call.9 = f32[1,1,128,128]{2,3,1,0:T(8,128)S(1)} custom-call(f32[1,1,128,128]{3,2,1,0:T(8,128)S(1)} %fusion.8), custom_call_target="InvertDiagBlocksLowerTriangular" | custom-call | tf_op jit(solution)/shard_map/vmap(jit(_solve_triangular))/triangular_solve | solution.py:15
  423.7 1.4 convolution_bitcast_fusion.1
  425.1 0.1 copy.38
  425.2 12.1 %all_to_all.12 = f32[1,512,128]{2,0,1:T(1,128)S(1)} all-to-all(f32[1,512,128]{2,0,1:T(1,128)S(1)} %copy.38), channel_id=1, replica_groups=mesh['row'=4,'col'=8] {'col'}, dimensions={1} | all-to-all | bytes 524288 | tf_op jit(solution)/shard_map/all_to_all | solution.py:71
  437.4 0.7 copy.66
  (4 shorter events, 0.0 us)
Async XLA Ops:
  7.2 0.8 copy-start
  7.2 354.0 %copy-start.2 = (bf16[64,4096]{1,0:T(8,128)(2,1)S(1)}, bf16[64,4096]{1,0:T(8,128)(2,1)}, u32[]{:S(2)}) copy-start(bf16[64,4096]{1,0:T(8,128)(2,1)} %param.13) | copy-start | bytes 1572868
  7.2 48.8 %all-reduce.8.cloned.1.call-start = ((), (), s32[]{:S(2)}) async-start(), calls=%async_computation.2 | async-start | bytes 131072 | tf_op jit(solution)/shard_map/psum | solution.py:11
  9.7 103.9 %all-reduce.10.cloned.1.call-start = ((), (), s32[]{:S(2)}) async-start(), calls=%async_computation.3 | async-start | bytes 131072 | tf_op jit(solution)/shard_map/psum | solution.py:36
  57.8 0.6 copy-start.1
  58.5 98.9 %all-reduce.12.cloned.1.call-start = ((), (), s32[]{:S(2)}) async-start(), calls=%async_computation.4 | async-start | bytes 131072 | tf_op jit(solution)/shard_map/psum | solution.py:11
  115.4 99.5 %all-reduce.14.cloned.1.call-start = ((), (), s32[]{:S(2)}) async-start(), calls=%async_computation.5 | async-start | bytes 131072 | tf_op jit(solution)/shard_map/psum | solution.py:36
  158.2 100.3 %all-reduce.16.cloned.1.call-start = ((), (), s32[]{:S(2)}) async-start(), calls=%async_computation.6 | async-start | bytes 131072 | tf_op jit(solution)/shard_map/psum | solution.py:11
  216.6 99.4 %all-reduce.18.cloned.1.call-start = ((), (), s32[]{:S(2)}) async-start(), calls=%async_computation.7 | async-start | bytes 131072 | tf_op jit(solution)/shard_map/psum | solution.py:36
  259.3 101.0 %all-reduce.20.cloned.1.call-start = ((), (), s32[]{:S(2)}) async-start(), calls=%async_computation.8 | async-start | bytes 131072 | tf_op jit(solution)/shard_map/psum | solution.py:11
  317.7 81.6 %reduce-scatter.2.cloned.1.call-start = ((), (), s32[]{:S(2)}) async-start(), calls=%async_computation.9 | async-start | bytes 2359296 | tf_op jit(solution)/shard_map/reduce_scatter | solution.py:63
  361.1 1.8 copy-start.3
Sparse Core Ops, SparseCore 0:
  11.4 44.5 all-reduce.7
  58.9 54.6 all-reduce.9
  116.5 40.8 all-reduce.11
  160.1 54.6 all-reduce.13
  217.6 40.8 all-reduce.15
  261.2 54.6 all-reduce.17
  319.4 40.8 all-reduce.19
  363.1 36.2 reduce-scatter.1
where the time goes:
time: 446 us; the launch traced here: 445 us
  waiting for transfers between devices  377 us (85%)
  other arithmetic  23.7 us (5%)
  between operations  14.3 us (3%)
  matrix products  12.4 us (3%)
  blocking collectives  12.1 us (3%)
  local copies, waits for them, and re-layouts  4.6 us (1%)
    psum x4, waiting for transfers between devices, from_root(): return lax.psum(block, axis)  173 us
    psum x3, waiting for transfers between devices, local(): summed = lax.psum(partial_value, 'col')  168 us
    reduce_scatter x1, waiting for transfers between devices, local(): lax.psum_scatter(jnp.einsum('kts,kr->tsr', cov_tiles, solved_low, preferr...  36.4 us
    another operation x3, other arithmetic, finish_tiles(): lower = jnp.linalg.cholesky(gram)  12.4 us
    all_to_all x1, blocking collectives, local(): lax.all_to_all(tile_bases, 'col', split_axis=1, concat_axis=0, tiled=True)  12.1 us
    another operation x2, other arithmetic, tile_basis(): return jax.scipy.linalg.solve_triangular(lower, tile.T, lower=True).T  10.5 us
  transfers between devices with their start and end apart: 8, of which 8 were waited for; matrix products, arithmetic and copies ran while one was open for 0% of the time, Pallas kernels for 0%

commit v1 on v0

--- a/solution.py
+++ b/solution.py
@@ -33,7 +33,7 @@
     partial_value = jnp.zeros((block_rows, rank_width), jnp.float32)
     own_solved = jnp.zeros((col_width, rank_width), jnp.float32)
     for block_index in range(row_count):
-        summed = lax.psum(partial_value, "col")
+        summed = jnp.sum(lax.all_gather(partial_value, "col"), axis=0)
         remaining = right_side - summed
         solved_full = jnp.dot(
             diag_inverse,

time: 446 us -> 317 us (0.71)
  waiting for transfers between devices: 377 us -> 207 us
  blocking collectives: 12.1 us -> 57.4 us
    psum x3 -> x0, waiting for transfers between devices: 168 us -> none  [local(): summed = lax.psum(partial_value, 'col')]
    all_gather x0 -> x3, blocking collectives: none -> 45.2 us  [local(): summed = jnp.sum(lax.all_gather(partial_value, 'col'), axis=0)]
  transfers between devices with their start and end apart: 8 -> 5, of which waited for: 8 -> 5; matrix products, arithmetic and copies ran while one was open for 0% -> 0% of each run, Pallas kernels for 0% -> 0%
where the time goes in v1:
time: 317 us
  waiting for transfers between devices  207 us (65%)
  blocking collectives  57.4 us (18%)
  other arithmetic  23.7 us (7%)
  between operations  14 us (4%)
  matrix products  10.7 us (3%)
  local copies, waits for them, and re-layouts  4.06 us (1%)
    psum x4, waiting for transfers between devices, from_root(): return lax.psum(block, axis)  170 us
    all_gather x3, blocking collectives, local(): summed = jnp.sum(lax.all_gather(partial_value, 'col'), axis=0)  45.2 us
    reduce_scatter x1, waiting for transfers between devices, local(): lax.psum_scatter(jnp.einsum('kts,kr->tsr', cov_tiles, solved_low, preferr...  36.3 us
    another operation x3, other arithmetic, finish_tiles(): lower = jnp.linalg.cholesky(gram)  12.4 us
    all_to_all x1, blocking collectives, local(): lax.all_to_all(tile_bases, 'col', split_axis=1, concat_axis=0, tiled=True)  12.1 us
    another operation x2, other arithmetic, tile_basis(): return jax.scipy.linalg.solve_triangular(lower, tile.T, lower=True).T  10.5 us
  transfers between devices with their start and end apart: 5, of which 5 were waited for; matrix products, arithmetic and copies ran while one was open for 0% of the time, Pallas kernels for 0%

profile of v1, /device:TPU:0, one launch (start us, length us, event | category | flops | bytes accessed | tf_op | source)
XLA Modules:
  0.0 316.7 jit_solution(8312312381166265246)
XLA Ops:
  7.2 0.0 copy-start
  7.2 0.0 copy-start.1
  7.2 0.0 all-reduce.5.cloned.1.call-start
  7.2 0.8 copy-done
  8.0 1.7 convolution_select_fusion.3
  9.7 0.0 all-reduce.5.cloned.1.call-update
  9.7 0.0 all-reduce.7.cloned.1.call-start
  9.8 46.2 %all-reduce.5.cloned.1.call-done = f32[128,128]{1,0:T(8,128)} async-done(((f32[128,128]{1,0:T(8,128)}), f32[128,128]{1,0:T(8,128)}) %all-reduce.5.cloned.1.call-update) | async-done | bytes 65552 | tf_op jit(solution)/shard_map/psum | solution.py:11
  56.0 0.8 constant_dynamic-slice_fusion.2
  56.8 1.0 conditional.3
  56.8 1.0 fusion.16
  57.8 14.7 %all-gather = f32[1024,128]{1,0:T(8,128)S(1)} all-gather(f32[128,128]{1,0:T(8,128)S(1)} %get-tuple-element.67), channel_id=2, replica_groups=mesh['row'=4,'col'=8] {'col'}, dimensions={0}, use_global_device_ids=true | all-gather | bytes 589824 | tf_op jit(solution)/shard_map/all_gather | solution.py:36
  72.6 0.0 copy-start.4
  72.6 0.0 copy-start.2
  72.6 1.7 fusion.2
  74.3 0.0 all-reduce.7.cloned.1.call-update
  74.3 0.0 all-reduce.9.cloned.1.call-start
  74.4 41.1 %all-reduce.7.cloned.1.call-done = f32[128,128]{1,0:T(8,128)} async-done(((f32[128,128]{1,0:T(8,128)}), f32[128,128]{1,0:T(8,128)}) %all-reduce.7.cloned.1.call-update) | async-done | bytes 65552 | tf_op jit(solution)/shard_map/psum | solution.py:11
  115.5 0.0 copy-start.5
  115.5 0.8 constant_dynamic-slice_fusion.1
  116.3 14.8 %all-gather.1 = f32[1024,128]{1,0:T(8,128)S(1)} all-gather(f32[128,128]{1,0:T(8,128)S(1)} %get-tuple-element.68), channel_id=3, replica_groups=mesh['row'=4,'col'=8] {'col'}, dimensions={0}, use_global_device_ids=true | all-gather | bytes 589824 | tf_op jit(solution)/shard_map/all_gather | solution.py:36
  131.1 0.0 copy-done.1
  131.1 0.8 fusion.1
  131.9 0.0 all-reduce.9.cloned.1.call-update
  132.0 0.0 all-reduce.11.cloned.1.call-start
  132.0 42.0 %all-reduce.9.cloned.1.call-done = f32[128,128]{1,0:T(8,128)} async-done(((f32[128,128]{1,0:T(8,128)}), f32[128,128]{1,0:T(8,128)}) %all-reduce.9.cloned.1.call-update) | async-done | bytes 65552 | tf_op jit(solution)/shard_map/psum | solution.py:11
  174.0 0.8 constant_dynamic-slice_fusion
  174.8 15.8 %all-gather.2 = f32[1024,128]{1,0:T(8,128)S(1)} all-gather(f32[128,128]{1,0:T(8,128)S(1)} %get-tuple-element.69), channel_id=4, replica_groups=mesh['row'=4,'col'=8] {'col'}, dimensions={0}, use_global_device_ids=true | all-gather | bytes 589824 | tf_op jit(solution)/shard_map/all_gather | solution.py:36
  190.6 0.8 fusion
  191.4 0.0 all-reduce.11.cloned.1.call-update
  191.5 0.0 reduce-scatter.2.cloned.1.call-start
  191.5 41.0 %all-reduce.11.cloned.1.call-done = f32[128,128]{1,0:T(8,128)} async-done(((f32[128,128]{1,0:T(8,128)}), f32[128,128]{1,0:T(8,128)}) %all-reduce.11.cloned.1.call-update) | async-done | bytes 65552 | tf_op jit(solution)/shard_map/psum | solution.py:11
  232.5 0.0 copy-done.4
  232.5 0.0 copy-done.5
  232.5 0.8 select_select_fusion.1
  233.3 0.0 copy-start.3
  233.3 0.0 copy-done.2
  233.3 1.8 convolution_bitcast_fusion
  235.1 0.0 reduce-scatter.2.cloned.1.call-update
  235.1 0.0 copy-done.3
  235.2 36.3 %reduce-scatter.2.cloned.1.call-done = f32[1,512,128]{1,2,0:T(8,128)} async-done(((f32[8,512,128]{1,2,0:T(8,128)}), f32[1,512,128]{1,2,0:T(8,128)}) %reduce-scatter.2.cloned.1.call-update) | async-done | bytes 262160 | tf_op jit(solution)/shard_map/reduce_scatter | solution.py:63
  271.4 1.4 fusion.6
  272.8 0.1 copy.37
  272.9 11.7 %custom-call.8 = f32[1,128,128]{2,1,0:T(8,128)S(1)} custom-call(f32[1,128,128]{2,1,0:T(8,128)S(1)} %fusion.9), custom_call_target="Cholesky" | custom-call | tf_op jit(solution)/shard_map/jit(cholesky)/cholesky | solution.py:19
  284.7 0.6 compare_reduce_fusion
  285.3 0.7 fusion.8
  286.0 9.8 %custom-call.9 = f32[1,1,128,128]{2,3,1,0:T(8,128)S(1)} custom-call(f32[1,1,128,128]{3,2,1,0:T(8,128)S(1)} %fusion.8), custom_call_target="InvertDiagBlocksLowerTriangular" | custom-call | tf_op jit(solution)/shard_map/vmap(jit(_solve_triangular))/triangular_solve | solution.py:15
  295.8 1.4 convolution_bitcast_fusion.1
  297.2 0.1 copy.38
  297.3 12.1 %all_to_all.12 = f32[1,512,128]{2,0,1:T(1,128)S(1)} all-to-all(f32[1,512,128]{2,0,1:T(1,128)S(1)} %copy.38), channel_id=1, replica_groups=mesh['row'=4,'col'=8] {'col'}, dimensions={1} | all-to-all | bytes 524288 | tf_op jit(solution)/shard_map/all_to_all | solution.py:71
  309.4 0.7 copy.66
  (7 shorter events, 0.1 us)
Async XLA Ops:
  7.2 0.8 copy-start
  7.2 123.9 %copy-start.1 = (f32[128,128]{1,0:T(8,128)S(1)}, f32[128,128]{1,0:T(8,128)}, u32[]{:S(2)}) copy-start(f32[128,128]{1,0:T(8,128)} %param.10) | copy-start | bytes 196612
  7.2 48.8 %all-reduce.5.cloned.1.call-start = ((), (), s32[]{:S(2)}) async-start(), calls=%async_computation.2 | async-start | bytes 131072 | tf_op jit(solution)/shard_map/psum | solution.py:11
  9.7 105.8 %all-reduce.7.cloned.1.call-start = ((), (), s32[]{:S(2)}) async-start(), calls=%async_computation.3 | async-start | bytes 131072 | tf_op jit(solution)/shard_map/psum | solution.py:11
  72.6 159.9 %copy-start.4 = (f32[128,128]{1,0:T(8,128)S(1)}, f32[128,128]{1,0:T(8,128)}, u32[]{:S(2)}) copy-start(f32[128,128]{1,0:T(8,128)} %all-reduce.5.cloned.1.call-done) | copy-start | bytes 196612
  72.6 160.7 %copy-start.2 = (bf16[64,4096]{1,0:T(8,128)(2,1)S(1)}, bf16[64,4096]{1,0:T(8,128)(2,1)}, u32[]{:S(2)}) copy-start(bf16[64,4096]{1,0:T(8,128)(2,1)} %param.13) | copy-start | bytes 1572868
  74.3 99.7 %all-reduce.9.cloned.1.call-start = ((), (), s32[]{:S(2)}) async-start(), calls=%async_computation.4 | async-start | bytes 131072 | tf_op jit(solution)/shard_map/psum | solution.py:11
  115.5 117.0 %copy-start.5 = (f32[128,128]{1,0:T(8,128)S(1)}, f32[128,128]{1,0:T(8,128)}, u32[]{:S(2)}) copy-start(f32[128,128]{1,0:T(8,128)} %all-reduce.7.cloned.1.call-done) | copy-start | bytes 196612
  132.0 100.5 %all-reduce.11.cloned.1.call-start = ((), (), s32[]{:S(2)}) async-start(), calls=%async_computation.5 | async-start | bytes 131072 | tf_op jit(solution)/shard_map/psum | solution.py:11
  191.5 80.0 %reduce-scatter.2.cloned.1.call-start = ((), (), s32[]{:S(2)}) async-start(), calls=%async_computation.6 | async-start | bytes 2359296 | tf_op jit(solution)/shard_map/reduce_scatter | solution.py:63
  233.3 1.9 copy-start.3
Sparse Core Ops, SparseCore 0:
  11.4 44.5 all-reduce.4
  74.5 40.9 all-reduce.6
  132.1 41.8 all-reduce.8
  191.6 40.8 all-reduce.10
  235.3 36.0 reduce-scatter.1
